TPU v7x, 256 devices: a whole 4x4x8 slice. The times are simulated.
256 devices in a mesh: group: 32 (over y, z), pencil: 8 (over x, core).
Axes of the slice: x: 4, y: 4, z: 8, core: 2. Of those that a mesh axis runs over, the one named last changes fastest.
Arguments:
- mult_iterate: float32 [32, 8, 8192], P('group', 'pencil'), may hold values from -6 to 6
- residual: float32 [32, 8, 8192], P('group', 'pencil'), may hold values from -6 to 6
- direction: float32 [32, 8, 8192], P('group', 'pencil'), may hold values from -6 to 6
- mult_scale: float32 [32, 8, 8192], P('group', 'pencil'), may hold values from 0.5 to 18
- eigen_basis: float32 [128, 3, 64, 64], P('group'), may hold values from -1 to 1
- eigen_values: float32 [128, 3, 64], P('group'), may hold values from 0.2 to 2
- elastic_coef: float32 [128, 3, 3], P('group'), may hold values from 0.5 to 2
- coarse_inverse: float32 [1024, 1024], replicated, may hold values from -1 to 2.5
- send_pos: int32 [32, 8, 16384], P('group', 'pencil'), may hold values from 0 to 24191, as said below
- pair_slots: int32 [32, 8, 2, 8192], P('group', 'pencil'), may hold values from 0 to 16383, as said below
- prim_rows: int32 [32, 8, 32], P('group', 'pencil'), may hold values from 0 to 16383, as said below
- coarse_idx: int32 [32, 8, 32], P('group', 'pencil'), may hold values from 0 to 1023
Outputs:
- new_iterate: float32 [32, 8, 8192], P('group', 'pencil')
- new_residual: float32 [32, 8, 8192], P('group', 'pencil')
- new_direction: float32 [32, 8, 8192], P('group', 'pencil')
Inputs may be any that keep to these rules, and one draw needn't show every extreme that they name: `send_pos`: distinct within each block (g, s). `pair_slots`: in each block (g, s) the two rows together hold every number of 0 to 16383 once. `prim_rows`: distinct within each block (g, s).
All inputs are finite; a program needn't handle non-finite values.
Results may differ from a plain program's by a relative error of at most 0.0003.
Values sent between devices are 32-bit elements; how exact they have to be, the bound alone decides.
No kernel may reach another device: no remote copies, remote signals or barrier semaphores. Data moves between devices by JAX's collectives and lax.ppermute only.
A program may use at most 128 MiB of HBM per device.

v0:
```python
import jax
import jax.numpy as jnp
from jax import lax
from jax.sharding import PartitionSpec as P


def cycle_slot(index, extent):
    cycle_size = 4 * extent - 4
    plane_index = index // cycle_size
    cycle_spot = index % cycle_size
    side_slot = jnp.where(
        cycle_spot < extent,
        cycle_spot,
        jnp.where(
            cycle_spot < 2 * extent - 2,
            cycle_spot + 1,
            jnp.where(cycle_spot < 3 * extent - 4, cycle_spot + 3, cycle_spot + 4),
        ),
    )
    return plane_index * 4 * extent + side_slot


def cycle_to_volume(cycles, extent):
    sides = cycles.reshape(cycles.shape[:-1] + (4, extent))
    count = jnp.arange(extent, dtype=jnp.int32)
    first_edge = (count == 0).astype(jnp.float32)
    last_edge = (count == extent - 1).astype(jnp.float32)
    plane = sides[..., 0, None, :] * first_edge[:, None]
    plane = plane + sides[..., 1, :, None] * first_edge[None, :]
    plane = plane + sides[..., 2, :, None] * last_edge[None, :]
    return plane + sides[..., 3, None, :] * last_edge[:, None]


def volume_to_cycle(volume):
    sides = jnp.stack(
        [volume[..., 0, :], volume[..., :, 0], volume[..., :, -1], volume[..., -1, :]], axis=-2
    )
    return sides.reshape(volume.shape[:-2] + (4 * volume.shape[-1],))


def spectrum(coeffs, along_x, along_y, along_z):
    first = coeffs[None, :, :, 0, None, None] * along_x.T[:, :, None, None, None]
    second = coeffs[None, :, :, 1, None, None] * along_y[None, :, None, :, None]
    third = coeffs[None, :, :, 2, None, None] * along_z[None, :, None, None, :]
    return first + second + third


def forward_yz(volume, basis):
    highest = lax.Precision.HIGHEST
    step_one = jnp.einsum("xpcyz,pzk->xpcyk", volume, basis[:, 2], precision=highest)
    return jnp.einsum("xpcyk,pyj->xpcjk", step_one, basis[:, 1], precision=highest)


def backward_yz(volume, basis):
    highest = lax.Precision.HIGHEST
    step_one = jnp.einsum("xpcjk,pyj->xpcyk", volume, basis[:, 1], precision=highest)
    return jnp.einsum("xpcyk,pzk->xpcyz", step_one, basis[:, 2], precision=highest)


def load_slab(arrived_rows, positions, slab_shape):
    cycle_total = slab_shape[0] * slab_shape[1] * slab_shape[2] * 4 * slab_shape[3]
    cycles = jnp.zeros((cycle_total,), jnp.float32).at[positions].set(arrived_rows)
    cycles = cycles.reshape(slab_shape[0], slab_shape[1], slab_shape[2], 4 * slab_shape[3])
    return cycle_to_volume(cycles, slab_shape[3])


def apply_inverse(arrived_rows, cycle_cells, basis, values, coeffs):
    highest = lax.Precision.HIGHEST
    pencils = lax.axis_size("pencil")
    extent = basis.shape[-1]
    patches = basis.shape[0]
    components = coeffs.shape[1]
    slab_x = extent // pencils
    slab_shape = (slab_x, patches, components, extent, extent)
    my_slab = lax.axis_index("pencil")
    row_start = my_slab * slab_x
    positions = cycle_slot(cycle_cells, extent)
    partial_yz = forward_yz(load_slab(arrived_rows, positions, slab_shape), basis)
    columns = lax.all_to_all(
        partial_yz.reshape(slab_x, patches, components, extent * extent),
        "pencil",
        split_axis=3,
        concat_axis=0,
        tiled=True,
    )
    columns = columns.reshape(extent, patches, components, slab_x, extent)
    spectral = jnp.einsum("xpcjk,pxi->ipcjk", columns, basis[:, 0], precision=highest)
    along_y = lax.dynamic_slice_in_dim(values[:, 1], row_start, slab_x, 1)
    scaled = spectral / spectrum(coeffs, values[:, 0], along_y, values[:, 2])
    mixed = jnp.einsum("ipcjk,pxi->xpcjk", scaled, basis[:, 0], precision=highest)
    mixed = mixed.reshape(extent, patches, components, slab_x * extent)
    back_x = lax.all_to_all(mixed, "pencil", split_axis=0, concat_axis=3, tiled=True).reshape(
        slab_shape
    )
    displace = backward_yz(back_x, basis)
    return volume_to_cycle(displace).reshape(-1)[positions]


def body(
    mult_iterate,
    residual,
    direction,
    mult_scale,
    eigen_basis,
    eigen_values,
    elastic_coef,
    coarse_inverse,
    send_pos,
    pair_slots,
    prim_rows,
    coarse_idx,
):
    highest = lax.Precision.HIGHEST
    groups = lax.axis_size("group")
    iterate_now = mult_iterate[0, 0]
    resid_now = residual[0, 0]
    search_dir = direction[0, 0]
    scale_now = mult_scale[0, 0]
    pair_rows = pair_slots[0, 0]
    cycle_cells = send_pos[0, 0]
    primal = prim_rows[0, 0]
    coarse_ids = coarse_idx[0, 0]
    rows_count = cycle_cells.shape[0]
    per_owner = rows_count // groups
    coarse_count = coarse_inverse.shape[0]
    old_part = jnp.sum(resid_now * scale_now * resid_now)
    old_norm = lax.psum(old_part, ("group", "pencil"))
    back_rows = (
        jnp.zeros((rows_count,), jnp.float32)
        .at[pair_rows[0]]
        .set(search_dir)
        .at[pair_rows[1]]
        .set(-search_dir)
    )
    arrived_rows = lax.all_to_all(
        back_rows.reshape(groups, per_owner), "group", split_axis=0, concat_axis=0, tiled=True
    ).reshape(rows_count)
    picked = apply_inverse(arrived_rows, cycle_cells, eigen_basis, eigen_values, elastic_coef)
    onehot = (coarse_ids[:, None] == jnp.arange(coarse_count, dtype=jnp.int32)[None, :]).astype(
        jnp.float32
    )
    local_coarse = jnp.dot(picked[primal], onehot, precision=highest)
    total_coarse = lax.psum(local_coarse, ("group", "pencil"))
    lifted = jnp.dot(coarse_inverse, total_coarse, precision=highest)
    sent_rows = picked.at[primal].add(jnp.dot(onehot, lifted, precision=highest))
    owner_rows = lax.all_to_all(
        sent_rows.reshape(groups, per_owner), "group", split_axis=0, concat_axis=0, tiled=True
    ).reshape(rows_count)
    mapped = owner_rows[pair_rows[0]] - owner_rows[pair_rows[1]]
    curvature = lax.psum(jnp.sum(search_dir * mapped), ("group", "pencil"))
    step_size = old_norm / curvature
    iterate_next = iterate_now + step_size * search_dir
    resid_next = resid_now - step_size * mapped
    precond = scale_now * resid_next
    norm_next = lax.psum(jnp.sum(resid_next * precond), ("group", "pencil"))
    search_next = precond + norm_next / old_norm * search_dir
    return (iterate_next[None, None], resid_next[None, None], search_next[None, None])


def solution(mesh):
    in_specs = (
        P("group", "pencil", None),
        P("group", "pencil", None),
        P("group", "pencil", None),
        P("group", "pencil", None),
        P("group", None, None, None),
        P("group", None, None),
        P("group", None, None),
        P(),
        P("group", "pencil", None),
        P("group", "pencil", None, None),
        P("group", "pencil", None),
        P("group", "pencil", None),
    )
    out_specs = (P("group", "pencil", None), P("group", "pencil", None), P("group", "pencil", None))
    return jax.shard_map(body, mesh=mesh, in_specs=in_specs, out_specs=out_specs, check_vma=False)
```

profile of v0, /device:TPU:1, one launch (start us, length us, event | category | flops | bytes accessed | tf_op | source)
XLA Modules:
  0.0 876.2 jit_solution(14388846261782737221)
XLA Ops:
  2.4 31.2 %scatter_custom_fusion = f32[16384]{0:T(1024)} fusion(s32[8192]{0:T(1024)S(1)} %bitcast.164, f32[8192]{0:T(1024)} %bitcast.154, f32[]{:T(128)} %constant.16.clone.1), kind=kCustom, calls=%fused_computation.81 | custom fusion | bytes 66048 | tf_op jit(solution)/shard_map/scatter | solution.py:131
  33.7 31.9 %scatter_fusion = f32[16384]{0:T(1024)} fusion(f32[16384]{0:T(1024)} %scatter_custom_fusion, s32[8192]{0:T(1024)S(1)} %bitcast.151, f32[8192]{0:T(1024)S(1)} %neg.3), kind=kCustom, calls=%fused_computation.5 | custom fusion | bytes 131072 | tf_op jit(solution)/shard_map/scatter | solution.py:133
  65.6 12.0 %all-to-all-start = ((f32[32,1,512]{2,1,0:T(1,128)}), f32[32,1,512]{2,1,0:T(1,128)S(1)}, u32[]{:S(2)}, u32[]{:S(2)}) async-start(f32[32,1,512]{2,1,0:T(1,128)} %bitcast.11), calls=%async_computation | async-start | bytes 131072 | tf_op jit(solution)/shard_map/all_to_all | solution.py:135
  78.5 8.0 all-to-all-done
  86.5 60.8 %scatter_custom_fusion.2 = f32[24576]{0:T(1024)S(1)} fusion(s32[16384]{0:T(1024)S(1)} %bitcast.160, f32[16384]{0:T(1024)S(1)} %bitcast.167, f32[]{:T(128)} %constant.16.clone.1), kind=kCustom, calls=%fused_computation.72 | custom fusion | bytes 98308 | tf_op jit(solution)/shard_map/scatter | solution.py:62
  151.7 5.2 fusion.16
  156.9 34.6 %copy.135 = f32[8,4,3,64,64]{0,1,2,4,3:T(4,128)} copy(f32[8,4,3,64,64]{3,4,2,0,1:T(8,128)S(1)} %fusion.16) | data formatting | bytes 3145728 | tf_op jit(solution)/shard_map/reshape | solution.py:80
  191.5 31.9 %reshape.387 = f32[8,1,49152]{2,1,0:T(1,128)} reshape(f32[4096,3,4,8]{3,2,1,0:T(4,128)} %bitcast.146) | data formatting | bytes 3145728
  223.4 6.5 all-to-all-start.1
  231.3 19.2 %all-to-all-done.1 = f32[8,1,49152]{2,1,0:T(1,128)S(1)} async-done(((f32[8,1,49152]{2,1,0:T(1,128)}), f32[8,1,49152]{2,1,0:T(1,128)S(1)}, u32[]{:S(2)}, u32[]{:S(2)}) %all-to-all-start.1) | async-done | bytes 1572896 | tf_op jit(solution)/shard_map/all_to_all | solution.py:79
  255.4 38.7 %reshape.388 = f32[4096,3,4,8]{3,2,1,0:T(4,128)} reshape(f32[8,49152]{1,0:T(8,128)S(1)} %reduce) | data formatting | bytes 3145728
  294.1 20.7 %copy.137 = f32[8,4,3,8,512]{4,0,3,2,1:T(8,128)} copy(f32[8,4,3,8,512]{0,1,2,4,3:T(4,128)} %bitcast.147) | data formatting | bytes 3145728 | tf_op jit(solution)/shard_map/all_to_all | solution.py:79
  317.4 5.1 fusion.5
  333.7 19.3 %all-to-all-done.2 = f32[64,4,3,512]{3,1,2,0:T(4,128)S(1)} async-done(((f32[64,4,3,512]{3,1,2,0:T(4,128)}), f32[64,4,3,512]{3,1,2,0:T(4,128)S(1)}, u32[]{:S(2)}, u32[]{:S(2)}) %all-to-all-start.2) | async-done | bytes 1572896 | tf_op jit(solution)/shard_map/all_to_all | solution.py:92
  358.3 5.1 fusion.35
  363.4 5.1 fusion.19
  375.9 160.4 %gather_fusion = f32[16384]{0:T(1024)} fusion(f32[24576]{0:T(1024)S(1)} %reshape_reshape.7, s32[16384]{0:T(1024)S(1)} %copy-done.8), kind=kCustom, calls=%fused_computation | custom fusion | bytes 196608 | tf_op jit(solution)/shard_map/gather | solution.py:96
  538.1 72.8 %psum.29 = f32[1024]{0:T(1024)S(1)} all-reduce(f32[1024]{0:T(1024)S(1)} %bitcast.172), channel_id=1, replica_groups=mesh['group'=32,'pencil'=8] {'group','pencil'}, use_global_device_ids=true, to_apply=%region_5.6 | all-reduce | flops 1024 | bytes 8192 | tf_op jit(solution)/shard_map/psum | solution.py:143
  610.9 5.6 convolution_bitcast_fusion
  624.7 8.2 all-to-all-done.3
  632.9 45.5 %gather_fusion.3 = f32[8192]{0:T(1024)S(1)} fusion(f32[16384]{0:T(1024)S(1)} %bitcast.144, s32[8192]{0:T(1024)S(1)} %copy-done.11), kind=kCustom, calls=%fused_computation.3 | custom fusion | bytes 98304 | tf_op jit(solution)/shard_map/gather | solution.py:149
  678.5 45.5 %gather_fusion.2 = f32[8192]{0:T(1024)S(1)} fusion(f32[16384]{0:T(1024)S(1)} %bitcast.145, s32[8192]{0:T(1024)S(1)} %broadcast_clamp_fusion.2), kind=kCustom, calls=%fused_computation.2 | custom fusion | bytes 98304 | tf_op jit(solution)/shard_map/gather | solution.py:149
  724.6 73.3 %all-reduce = (f32[]{:T(128)}, f32[]{:T(128)}) all-reduce(f32[]{:T(128)} %fusion.51, f32[]{:T(128)} %get-tuple-element.9), channel_id=1, replica_groups=mesh['group'=32,'pencil'=8] {'group','pencil'}, use_global_device_ids=true, to_apply=%region_1.0 | all-reduce | flops 2 | bytes 16 | tf_op jit(solution)/shard_map/psum | solution.py:127
  799.9 74.0 %psum.31 = f32[]{:T(128)} all-reduce(f32[]{:T(128)} %get-tuple-element.7), channel_id=1, replica_groups=mesh['group'=32,'pencil'=8] {'group','pencil'}, use_global_device_ids=true, to_apply=%region_10.11 | all-reduce | flops 1 | bytes 8 | tf_op jit(solution)/shard_map/psum | solution.py:155
  (93 shorter events, 51.4 us)
Async XLA Ops:
  1.6 64.0 %copy-start.1 = (s32[8192,1]{0,1:T(1,128)}, s32[8192,1]{0,1:T(1,128)S(1)}, u32[]{:S(2)}) copy-start(s32[8192,1]{0,1:T(1,128)S(1)} %get-tuple-element.19) | copy-start | bytes 98308
  1.6 63.9 %copy-start.9 = (s32[8192,1]{0,1:T(1,128)}, s32[8192,1]{0,1:T(1,128)S(1)}, u32[]{:S(2)}) copy-start(s32[8192,1]{0,1:T(1,128)S(1)} %get-tuple-element.20) | copy-start | bytes 98308
  33.7 44.0 %copy-start.12 = (s32[1,1,16384]{2,1,0:T(1,128)S(1)}, s32[1,1,16384]{2,1,0:T(1,128)}, u32[]{:S(2)}) copy-start(s32[1,1,16384]{2,1,0:T(1,128)} %param.20) | copy-start | bytes 196612
  33.7 114.0 %copy-start = (f32[4,3,64,64]{3,2,1,0:T(8,128)S(1)}, f32[4,3,64,64]{3,2,1,0:T(8,128)}, u32[]{:S(2)}) copy-start(f32[4,3,64,64]{3,2,1,0:T(8,128)} %param.16) | copy-start | bytes 589828
  65.6 20.9 %all-to-all-start = ((f32[32,1,512]{2,1,0:T(1,128)}), f32[32,1,512]{2,1,0:T(1,128)S(1)}, u32[]{:S(2)}, u32[]{:S(2)}) async-start(f32[32,1,512]{2,1,0:T(1,128)} %bitcast.11), calls=%async_computation | async-start | bytes 131072 | tf_op jit(solution)/shard_map/all_to_all | solution.py:135
  78.4 8.1 copy-start.6
  223.4 6.5 copy-start.13
  223.4 7.0 copy-start.16
  223.4 27.1 %all-to-all-start.1 = ((f32[8,1,49152]{2,1,0:T(1,128)}), f32[8,1,49152]{2,1,0:T(1,128)S(1)}, u32[]{:S(2)}, u32[]{:S(2)}) async-start(f32[8,1,49152]{2,1,0:T(1,128)} %reshape.387), calls=%async_computation.1 | async-start | bytes 3145728 | tf_op jit(solution)/shard_map/all_to_all | solution.py:79
  317.4 5.1 copy-start.14
  325.8 6.7 copy-start.17
  327.8 4.6 copy-start.2
  327.8 5.2 copy-start.7
  327.8 25.2 %all-to-all-start.2 = ((f32[64,4,3,512]{3,1,2,0:T(4,128)}), f32[64,4,3,512]{3,1,2,0:T(4,128)S(1)}, u32[]{:S(2)}, u32[]{:S(2)}) async-start(f32[64,4,3,512]{3,1,2,0:T(4,128)} %copy.119), calls=%async_computation.2 | async-start | bytes 3145728 | tf_op jit(solution)/shard_map/all_to_all | solution.py:92
  371.3 4.6 copy-start.8
  375.9 162.0 %copy-start.18 = (s32[1,1,32]{2,1,0:T(1,128)S(1)}, s32[1,1,32]{2,1,0:T(1,128)}, u32[]{:S(2)}) copy-start(s32[1,1,32]{2,1,0:T(1,128)} %param.23) | copy-start | bytes 388
  536.3 87.7 %copy-start.10 = (s32[8192,1]{0,1:T(1,128)S(1)}, s32[8192,1]{0,1:T(1,128)}, u32[]{:S(2)}) copy-start(s32[8192,1]{0,1:T(1,128)} %copy-done.9) | copy-start | bytes 98308
  536.3 87.7 %copy-start.4 = (f32[1,1,8192]{2,1,0:T(1,128)S(1)}, f32[1,1,8192]{2,1,0:T(1,128)}, u32[]{:S(2)}) copy-start(f32[1,1,8192]{2,1,0:T(1,128)} %param.15) | copy-start | bytes 98308
  536.3 87.7 %copy-start.5 = (f32[1,1,8192]{2,1,0:T(1,128)S(1)}, f32[1,1,8192]{2,1,0:T(1,128)}, u32[]{:S(2)}) copy-start(f32[1,1,8192]{2,1,0:T(1,128)} %param.13) | copy-start | bytes 98308
  536.3 96.6 %copy-start.11 = (s32[8192]{0:T(1024)S(1)}, s32[8192]{0:T(1024)}, u32[]{:S(2)}) copy-start(s32[8192]{0:T(1024)} %broadcast_clamp_fusion.1) | copy-start | bytes 98308
  619.0 13.9 %all-to-all-start.3 = ((f32[32,1,512]{2,1,0:T(1,128)}), f32[32,1,512]{2,1,0:T(1,128)S(1)}, u32[]{:S(2)}, u32[]{:S(2)}) async-start(f32[32,1,512]{2,1,0:T(1,128)} %bitcast.57), calls=%async_computation.3 | async-start | bytes 131072 | tf_op jit(solution)/shard_map/all_to_all | solution.py:146
  678.4 45.6 %copy-start.3 = (f32[1,1,8192]{2,1,0:T(1,128)S(1)}, f32[1,1,8192]{2,1,0:T(1,128)}, u32[]{:S(2)}) copy-start(f32[1,1,8192]{2,1,0:T(1,128)} %param.14) | copy-start | bytes 98308
  678.4 196.8 %copy-start.15 = (f32[1,1,8192]{2,1,0:T(1,128)S(1)}, f32[1,1,8192]{2,1,0:T(1,128)}, u32[]{:S(2)}) copy-start(f32[1,1,8192]{2,1,0:T(1,128)} %param.12) | copy-start | bytes 98308
where the time goes:
time: 881 us; the launch traced here: 876 us
  local copies, waits for them, and re-layouts  521 us (59%)
  blocking collectives  220 us (25%)
  waiting for transfers between devices  54.7 us (6%)
  matrix products  33.9 us (4%)
  starting transfers between devices  28.2 us (3%)
  other arithmetic  14.1 us (2%)
    gather x1, local copies, waits for them, and re-layouts, apply_inverse(): return volume_to_cycle(displace).reshape(-1)[positions]  160 us
    gather x2, local copies, waits for them, and re-layouts, body(): mapped = owner_rows[pair_rows[0]] - owner_rows[pair_rows[1]]  91.1 us
    psum x1, blocking collectives, body(): norm_next = lax.psum(jnp.sum(resid_next * precond), ('group', 'pencil'))  74 us
    psum x1, blocking collectives, body(): old_norm = lax.psum(old_part, ('group', 'pencil'))  73.3 us
    psum x1, blocking collectives, body(): total_coarse = lax.psum(local_coarse, ('group', 'pencil'))  72.8 us
    unnamed x40, local copies, waits for them, and re-layouts  70.6 us
    scatter x2, local copies, waits for them, and re-layouts, body(): back_rows = jnp.zeros((rows_count,), jnp.float32).at[pair_rows[0]].set(se...  63.2 us
    scatter x1, local copies, waits for them, and re-layouts, load_slab(): jnp.zeros((cycle_total,), jnp.float32).at[positions].set(arrived_rows)  60.8 us
  transfers between devices with their start and end apart: 4, of which 4 were waited for; matrix products, arithmetic and copies ran while one was open for 0% of the time, Pallas kernels for 0%

commit v1 on v0

--- a/solution.py
+++ b/solution.py
@@ -76,12 +76,20 @@
     row_start = my_slab * slab_x
     positions = cycle_slot(cycle_cells, extent)
     partial_yz = forward_yz(load_slab(arrived_rows, positions, slab_shape), basis)
-    columns = lax.all_to_all(
-        partial_yz.reshape(slab_x, patches, components, extent * extent),
-        "pencil",
-        split_axis=3,
-        concat_axis=0,
-        tiled=True,
+    columns = jnp.concatenate(
+        lax.all_to_all(
+            jnp.stack(
+                jnp.split(
+                    partial_yz.reshape(slab_x, patches, components, extent * extent),
+                    lax.axis_size("pencil"),
+                    axis=3,
+                )
+            ),
+            "pencil",
+            0,
+            0,
+        ),
+        axis=0,
     )
     columns = columns.reshape(extent, patches, components, slab_x, extent)
     spectral = jnp.einsum("xpcjk,pxi->ipcjk", columns, basis[:, 0], precision=highest)

time: 881 us -> 762 us (0.86)
  local copies, waits for them, and re-layouts: 521 us -> 406 us
    unnamed x40 -> x45, local copies, waits for them, and re-layouts: 70.6 us -> 4.92 us
    reshape x1, local copies, waits for them, and re-layouts: 34.6 us -> 2.42 us  [apply_inverse(): partial_yz.reshape(slab_x, patches, components, extent * extent)]
    all_to_all x2 -> x1, local copies, waits for them, and re-layouts: 21.2 us -> 1.32 us  [apply_inverse(): lax.all_to_all(jnp.stack(jnp.split(partial_yz.reshape(slab_x, patches, co...]
  transfers between devices with their start and end apart: 4 -> 4, of which waited for: 4 -> 4; matrix products, arithmetic and copies ran while one was open for 0% -> 1% of each run, Pallas kernels for 0% -> 0%
where the time goes in v1:
time: 762 us; the launch traced here: 757 us
  local copies, waits for them, and re-layouts  406 us (53%)
  blocking collectives  220 us (29%)
  waiting for transfers between devices  54.7 us (7%)
  matrix products  33.9 us (4%)
  starting transfers between devices  28.2 us (4%)
  other arithmetic  9.74 us (1%)
    gather x1, local copies, waits for them, and re-layouts, apply_inverse(): return volume_to_cycle(displace).reshape(-1)[positions]  160 us
    gather x2, local copies, waits for them, and re-layouts, body(): mapped = owner_rows[pair_rows[0]] - owner_rows[pair_rows[1]]  91.1 us
    psum x1, blocking collectives, body(): norm_next = lax.psum(jnp.sum(resid_next * precond), ('group', 'pencil'))  74 us
    psum x1, blocking collectives, body(): old_norm = lax.psum(old_part, ('group', 'pencil'))  73.3 us
    psum x1, blocking collectives, body(): total_coarse = lax.psum(local_coarse, ('group', 'pencil'))  72.8 us
    scatter x2, local copies, waits for them, and re-layouts, body(): back_rows = jnp.zeros((rows_count,), jnp.float32).at[pair_rows[0]].set(se...  63.1 us
    scatter x1, local copies, waits for them, and re-layouts, load_slab(): jnp.zeros((cycle_total,), jnp.float32).at[positions].set(arrived_rows)  60.9 us
    all_to_all x1, waiting for transfers between devices, apply_inverse(): lax.all_to_all(mixed, 'pencil', split_axis=0, concat_axis=3, tiled=True)  19.3 us
  transfers between devices with their start and end apart: 4, of which 4 were waited for; matrix products, arithmetic and copies ran while one was open for 1% of the time, Pallas kernels for 0%

profile of v1, /device:TPU:1, one launch (start us, length us, event | category | flops | bytes accessed | tf_op | source)
XLA Modules:
  0.0 757.2 jit_solution(11894205898412323725)
XLA Ops:
  2.4 31.2 %scatter_custom_fusion = f32[16384]{0:T(1024)} fusion(s32[8192]{0:T(1024)S(1)} %bitcast.191, f32[8192]{0:T(1024)} %bitcast.181, f32[]{:T(128)} %constant.16.clone.1), kind=kCustom, calls=%fused_computation.97 | custom fusion | bytes 66048 | tf_op jit(solution)/shard_map/scatter | solution.py:139
  33.7 31.9 %scatter_fusion = f32[16384]{0:T(1024)} fusion(f32[16384]{0:T(1024)} %scatter_custom_fusion, s32[8192]{0:T(1024)S(1)} %bitcast.178, f32[8192]{0:T(1024)S(1)} %neg.3), kind=kCustom, calls=%fused_computation.5 | custom fusion | bytes 131072 | tf_op jit(solution)/shard_map/scatter | solution.py:141
  65.6 12.0 %all-to-all-start = ((f32[32,1,512]{2,1,0:T(1,128)}), f32[32,1,512]{2,1,0:T(1,128)S(1)}, u32[]{:S(2)}, u32[]{:S(2)}) async-start(f32[32,1,512]{2,1,0:T(1,128)} %bitcast.11), calls=%async_computation | async-start | bytes 131072 | tf_op jit(solution)/shard_map/all_to_all | solution.py:143
  78.4 8.0 %all-to-all-done = f32[32,1,512]{2,1,0:T(1,128)S(1)} async-done(((f32[32,1,512]{2,1,0:T(1,128)}), f32[32,1,512]{2,1,0:T(1,128)S(1)}, u32[]{:S(2)}, u32[]{:S(2)}) %all-to-all-start) | async-done | bytes 65568 | tf_op jit(solution)/shard_map/all_to_all | solution.py:143
  86.5 60.9 %scatter_custom_fusion.2 = f32[24576]{0:T(1024)S(1)} fusion(s32[16384]{0:T(1024)S(1)} %bitcast.187, f32[16384]{0:T(1024)S(1)} %bitcast.194, f32[]{:T(128)} %constant.16.clone.1), kind=kCustom, calls=%fused_computation.88 | custom fusion | bytes 98308 | tf_op jit(solution)/shard_map/scatter | solution.py:62
  147.8 4.0 fusion.8
  151.9 5.2 fusion.16
  167.4 6.6 all-to-all-start.1
  175.4 19.1 %all-to-all-done.1 = f32[8,8,4,3,512]{4,1,3,2,0:T(8,128)S(1)} async-done(((f32[8,8,4,3,512]{4,1,3,2,0:T(8,128)}), f32[8,8,4,3,512]{4,1,3,2,0:T(8,128)S(1)}, u32[]{:S(2)}, u32[]{:S(2)}) %all-to-all-start.1) | async-done | bytes 1572896 | tf_op jit(solution)/shard_map/all_to_all | solution.py:80
  198.3 5.1 fusion.5
  203.4 3.2 fusion.2
  208.7 4.6 all-to-all-start.2
  214.6 19.3 %all-to-all-done.2 = f32[64,4,3,512]{3,1,2,0:T(4,128)S(1)} async-done(((f32[64,4,3,512]{3,1,2,0:T(4,128)}), f32[64,4,3,512]{3,1,2,0:T(4,128)S(1)}, u32[]{:S(2)}, u32[]{:S(2)}) %all-to-all-start.2) | async-done | bytes 1572896 | tf_op jit(solution)/shard_map/all_to_all | solution.py:100
  239.2 5.1 fusion.43
  244.3 5.1 fusion.19
  256.8 160.3 %gather_fusion = f32[16384]{0:T(1024)} fusion(f32[24576]{0:T(1024)S(1)} %reshape_reshape.11, s32[16384]{0:T(1024)S(1)} %copy-done.8), kind=kCustom, calls=%fused_computation | custom fusion | bytes 196608 | tf_op jit(solution)/shard_map/gather | solution.py:104
  418.9 72.8 %psum.29 = f32[1024]{0:T(1024)S(1)} all-reduce(f32[1024]{0:T(1024)S(1)} %bitcast.199), channel_id=1, replica_groups=mesh['group'=32,'pencil'=8] {'group','pencil'}, use_global_device_ids=true, to_apply=%region_5.6 | all-reduce | flops 1024 | bytes 8192 | tf_op jit(solution)/shard_map/psum | solution.py:151
  491.7 5.6 convolution_bitcast_fusion
  499.8 5.0 all-to-all-start.3
  505.4 8.2 %all-to-all-done.3 = f32[32,1,512]{2,1,0:T(1,128)S(1)} async-done(((f32[32,1,512]{2,1,0:T(1,128)}), f32[32,1,512]{2,1,0:T(1,128)S(1)}, u32[]{:S(2)}, u32[]{:S(2)}) %all-to-all-start.3) | async-done | bytes 65568 | tf_op jit(solution)/shard_map/all_to_all | solution.py:154
  513.7 45.5 %gather_fusion.3 = f32[8192]{0:T(1024)S(1)} fusion(f32[16384]{0:T(1024)S(1)} %bitcast.174, s32[8192]{0:T(1024)S(1)} %copy-done.11), kind=kCustom, calls=%fused_computation.3 | custom fusion | bytes 98304 | tf_op jit(solution)/shard_map/gather | solution.py:157
  559.2 45.5 %gather_fusion.2 = f32[8192]{0:T(1024)S(1)} fusion(f32[16384]{0:T(1024)S(1)} %bitcast.175, s32[8192]{0:T(1024)S(1)} %broadcast_clamp_fusion.2), kind=kCustom, calls=%fused_computation.2 | custom fusion | bytes 98304 | tf_op jit(solution)/shard_map/gather | solution.py:157
  605.4 73.3 %all-reduce = (f32[]{:T(128)}, f32[]{:T(128)}) all-reduce(f32[]{:T(128)} %fusion.59, f32[]{:T(128)} %get-tuple-element.9), channel_id=1, replica_groups=mesh['group'=32,'pencil'=8] {'group','pencil'}, use_global_device_ids=true, to_apply=%region_1.0 | all-reduce | flops 2 | bytes 16 | tf_op jit(solution)/shard_map/psum | solution.py:135
  680.6 74.0 %psum.31 = f32[]{:T(128)} all-reduce(f32[]{:T(128)} %get-tuple-element.7), channel_id=1, replica_groups=mesh['group'=32,'pencil'=8] {'group','pencil'}, use_global_device_ids=true, to_apply=%region_10.11 | all-reduce | flops 1 | bytes 8 | tf_op jit(solution)/shard_map/psum | solution.py:163
  (98 shorter events, 41.1 us)
Async XLA Ops:
  1.6 64.0 %copy-start.1 = (s32[8192,1]{0,1:T(1,128)}, s32[8192,1]{0,1:T(1,128)S(1)}, u32[]{:S(2)}) copy-start(s32[8192,1]{0,1:T(1,128)S(1)} %get-tuple-element.19) | copy-start | bytes 98308
  1.6 63.9 %copy-start.9 = (s32[8192,1]{0,1:T(1,128)}, s32[8192,1]{0,1:T(1,128)S(1)}, u32[]{:S(2)}) copy-start(s32[8192,1]{0,1:T(1,128)S(1)} %get-tuple-element.20) | copy-start | bytes 98308
  33.7 44.0 %copy-start.12 = (s32[1,1,16384]{2,1,0:T(1,128)S(1)}, s32[1,1,16384]{2,1,0:T(1,128)}, u32[]{:S(2)}) copy-start(s32[1,1,16384]{2,1,0:T(1,128)} %param.20) | copy-start | bytes 196612
  33.7 114.2 %copy-start = (f32[4,3,64,64]{3,2,1,0:T(8,128)S(1)}, f32[4,3,64,64]{3,2,1,0:T(8,128)}, u32[]{:S(2)}) copy-start(f32[4,3,64,64]{3,2,1,0:T(8,128)} %param.16) | copy-start | bytes 589828
  65.6 20.9 %all-to-all-start = ((f32[32,1,512]{2,1,0:T(1,128)}), f32[32,1,512]{2,1,0:T(1,128)S(1)}, u32[]{:S(2)}, u32[]{:S(2)}) async-start(f32[32,1,512]{2,1,0:T(1,128)} %bitcast.11), calls=%async_computation | async-start | bytes 131072 | tf_op jit(solution)/shard_map/all_to_all | solution.py:143
  78.4 8.1 %copy-start.6 = (s32[16384,1]{0,1:T(1,128)}, s32[16384,1]{0,1:T(1,128)S(1)}, u32[]{:S(2)}) copy-start(s32[16384,1]{0,1:T(1,128)S(1)} %compare_select_fusion) | copy-start | bytes 196612
  161.8 12.2 %copy-start.13 = (f32[4,3,3]{2,0,1:T(4,128)S(1)}, f32[4,3,3]{2,0,1:T(4,128)}, u32[]{:S(2)}) copy-start(f32[4,3,3]{2,0,1:T(4,128)} %param.18) | copy-start | bytes 436
  161.8 12.6 %copy-start.16 = (f32[4,3,64]{2,0,1:T(4,128)S(1)}, f32[4,3,64]{2,0,1:T(4,128)}, u32[]{:S(2)}) copy-start(f32[4,3,64]{2,0,1:T(4,128)} %param.17) | copy-start | bytes 9220
  167.4 27.2 %all-to-all-start.1 = ((f32[8,8,4,3,512]{4,1,3,2,0:T(8,128)}), f32[8,8,4,3,512]{4,1,3,2,0:T(8,128)S(1)}, u32[]{:S(2)}, u32[]{:S(2)}) async-start(f32[8,8,4,3,512]{4,1,3,2,0:T(8,128)} %fusion.33), calls=%async_computation.1 | async-start | bytes 3145728 | tf_op jit(solution)/shard_map/all_to_all | solution.py:80
  198.3 5.1 copy-start.14
  206.7 6.7 copy-start.17
  208.7 4.6 copy-start.2
  208.7 5.2 copy-start.7
  208.7 25.2 %all-to-all-start.2 = ((f32[64,4,3,512]{3,1,2,0:T(4,128)}), f32[64,4,3,512]{3,1,2,0:T(4,128)S(1)}, u32[]{:S(2)}, u32[]{:S(2)}) async-start(f32[64,4,3,512]{3,1,2,0:T(4,128)} %copy.115), calls=%async_computation.2 | async-start | bytes 3145728 | tf_op jit(solution)/shard_map/all_to_all | solution.py:100
  252.2 4.6 copy-start.8
  256.8 161.9 %copy-start.18 = (s32[1,1,32]{2,1,0:T(1,128)S(1)}, s32[1,1,32]{2,1,0:T(1,128)}, u32[]{:S(2)}) copy-start(s32[1,1,32]{2,1,0:T(1,128)} %param.23) | copy-start | bytes 388
  417.1 87.7 %copy-start.10 = (s32[8192,1]{0,1:T(1,128)S(1)}, s32[8192,1]{0,1:T(1,128)}, u32[]{:S(2)}) copy-start(s32[8192,1]{0,1:T(1,128)} %copy-done.9) | copy-start | bytes 98308
  417.1 87.7 %copy-start.4 = (f32[1,1,8192]{2,1,0:T(1,128)S(1)}, f32[1,1,8192]{2,1,0:T(1,128)}, u32[]{:S(2)}) copy-start(f32[1,1,8192]{2,1,0:T(1,128)} %param.15) | copy-start | bytes 98308
  417.1 87.7 %copy-start.5 = (f32[1,1,8192]{2,1,0:T(1,128)S(1)}, f32[1,1,8192]{2,1,0:T(1,128)}, u32[]{:S(2)}) copy-start(f32[1,1,8192]{2,1,0:T(1,128)} %param.13) | copy-start | bytes 98308
  417.1 96.6 %copy-start.11 = (s32[8192]{0:T(1024)S(1)}, s32[8192]{0:T(1024)}, u32[]{:S(2)}) copy-start(s32[8192]{0:T(1024)} %broadcast_clamp_fusion.1) | copy-start | bytes 98308
  499.8 13.9 %all-to-all-start.3 = ((f32[32,1,512]{2,1,0:T(1,128)}), f32[32,1,512]{2,1,0:T(1,128)S(1)}, u32[]{:S(2)}, u32[]{:S(2)}) async-start(f32[32,1,512]{2,1,0:T(1,128)} %bitcast.61), calls=%async_computation.3 | async-start | bytes 131072 | tf_op jit(solution)/shard_map/all_to_all | solution.py:154
  559.2 45.6 %copy-start.3 = (f32[1,1,8192]{2,1,0:T(1,128)S(1)}, f32[1,1,8192]{2,1,0:T(1,128)}, u32[]{:S(2)}) copy-start(f32[1,1,8192]{2,1,0:T(1,128)} %param.14) | copy-start | bytes 98308
  559.2 196.8 %copy-start.15 = (f32[1,1,8192]{2,1,0:T(1,128)S(1)}, f32[1,1,8192]{2,1,0:T(1,128)}, u32[]{:S(2)}) copy-start(f32[1,1,8192]{2,1,0:T(1,128)} %param.12) | copy-start | bytes 98308
